TPU v7x, 128 devices: a whole 4x4x4 slice. The times are simulated.
128 devices in a mesh: sub: 32 (over x, y, core), rep: 4 (over z).
Axes of the slice: x: 4, y: 4, z: 4, core: 2. Of those that a mesh axis runs over, the one named last changes fastest.
Arguments:
- loads: bfloat16 [256, 256, 1024], P('sub', 'rep'), may hold values from -6 to 6
- operators: bfloat16 [256, 1024, 1024], P('sub'), may hold values from -0.1875 to 0.1875
- owner: int32 [2048, 1], P('sub'), may hold values from 0 to 31; in each aligned block of 64 rows (0 to 63, 64 to 127, ...) at most 4 rows name the same one
- dual_block: int32 [2048], P('sub'), may hold values from 0 to 15
- scale_index: int32 [65536], P('sub'), may hold values from 0 to 3
- basis: bfloat16 [65536, 1024], P('sub'), may hold values from -0.0234375 to 0.0234375
- coarse: bfloat16 [1024, 1024], replicated, may hold values from -1.5 to 1.5
Outputs:
- start: float32 [256, 65536], P('rep', 'sub')
- resid: float32 [256, 65536], P('rep', 'sub')
Inputs may be any that keep to these rules, and one draw needn't show every extreme that they name: Among the blocks of the subdomains of one index of sub (aligned blocks of 64 rows), no owner is named more than 4 times, a bound that some block reaches.
All inputs are finite; a program needn't handle non-finite values.
Results may differ from a plain program's by a relative error of at most 0.0075.
Values may be sent and summed in bfloat16 or wider, within the bound.
No kernel may reach another device: no remote copies, remote signals or barrier semaphores. Data moves between devices by JAX's collectives and lax.ppermute only.
A program may use at most 128 MiB of HBM per device.

v0:
```python
import jax
import jax.numpy as jnp
from jax import lax
from jax.sharding import PartitionSpec as P

BLK = 128


def apply_local(inputs, operators):
    return jnp.einsum("skl,slm->skm", inputs, operators, preferred_element_type=jnp.float32).astype(
        jnp.bfloat16
    )


def make_blocks(values, width):
    count, columns, local = values.shape
    return (
        values.reshape(count, columns, local // width, width)
        .transpose(0, 2, 1, 3)
        .reshape(-1, columns, width)
    )


def from_blocks(blocks, count):
    total, columns, width = blocks.shape
    per_sub = total // count
    return (
        blocks.reshape(count, per_sub, columns, width)
        .transpose(0, 2, 1, 3)
        .reshape(count, columns, per_sub * width)
    )


def pack_slots(blocks, dests, ranks, peers, slots):
    columns, width = (blocks.shape[1], blocks.shape[2])
    return jnp.zeros((peers, slots, columns, width), jnp.bfloat16).at[dests, ranks].set(blocks)


def accumulate(received, got_ids, own_blocks, weight):
    columns, width = (received.shape[2], received.shape[3])
    flat = received.reshape(-1, columns, width).astype(jnp.float32)
    total = jnp.zeros((own_blocks, columns, width), jnp.float32).at[got_ids.reshape(-1)].add(flat)
    return total.transpose(1, 0, 2).reshape(columns, own_blocks * width) * weight[None, :]


def per_device(loads, operators, owner, dual_block, scale_index, basis, coarse):
    sub_count = loads.shape[0]
    width = BLK
    peers = lax.axis_size("sub")
    dests = owner[:, 0]
    nblocks = dests.shape[0]
    slots = max(2, 2 * nblocks // peers)
    own_blocks = basis.shape[0] // width
    positions = jnp.arange(nblocks, dtype=jnp.int32)
    earlier = positions[None, :] < positions[:, None]
    same = dests[None, :] == dests[:, None]
    ranks = jnp.sum(jnp.logical_and(earlier, same), axis=1)
    weight = 1.0 / (1.0 + scale_index.astype(jnp.float32))
    terms = apply_local(loads, operators)
    packed = pack_slots(make_blocks(terms, width), dests, ranks, peers, slots)
    id_slots = jnp.zeros((peers, slots), jnp.int32).at[dests, ranks].set(dual_block)
    received, got_ids = (
        lax.all_to_all(packed, "sub", split_axis=0, concat_axis=0, tiled=True),
        lax.all_to_all(id_slots, "sub", split_axis=0, concat_axis=0, tiled=True),
    )
    dual = accumulate(received, got_ids, own_blocks, weight)
    coeff = jnp.dot(dual.astype(jnp.bfloat16), basis, preferred_element_type=jnp.float32)
    summed = lax.psum(coeff, "sub")
    solved = jnp.dot(
        summed.astype(jnp.bfloat16), coarse, preferred_element_type=jnp.float32
    ).astype(jnp.bfloat16)
    start = lax.dot_general(
        solved, basis, (((1,), (1,)), ((), ())), preferred_element_type=jnp.float32
    )
    columns = start.shape[0]
    start_blocks = start.astype(jnp.bfloat16).reshape(columns, own_blocks, width).transpose(1, 0, 2)
    requested = start_blocks[got_ids]
    returned = lax.all_to_all(requested, "sub", split_axis=0, concat_axis=0, tiled=True)
    picked = returned[dests, ranks]
    local = from_blocks(picked, sub_count)
    again = apply_local(local, operators)
    received_again = lax.all_to_all(
        pack_slots(make_blocks(again, width), dests, ranks, peers, slots),
        "sub",
        split_axis=0,
        concat_axis=0,
        tiled=True,
    )
    applied = accumulate(received_again, got_ids, own_blocks, weight)
    return (start, dual - applied)


def solution(mesh):
    return jax.shard_map(
        per_device,
        mesh=mesh,
        in_specs=(
            P("sub", "rep", None),
            P("sub", None, None),
            P("sub", None),
            P("sub"),
            P("sub"),
            P("sub", None),
            P(),
        ),
        out_specs=(P("rep", "sub"), P("rep", "sub")),
        check_vma=False,
    )
```

profile of v0, /device:TPU:1, one launch (start us, length us, event | category | flops | bytes accessed | tf_op | source)
XLA Modules:
  0.0 336.0 jit_solution(8166071477639882503)
XLA Ops:
  0.6 0.0 copy-start
  0.6 1.0 convert_reduce_fusion
  1.6 0.7 fusion.15
  2.3 5.7 %scatter_fusion = s32[32,4]{0,1:T(4,128)S(1)} fusion(s32[32,4]{0,1:T(4,128)S(1)} %broadcast.75, s32[64]{0:T(128)S(1)} %get-tuple-element.2, s32[64]{0:T(128)} %param.10), kind=kCustom, calls=%fused_computation.2 | custom fusion | bytes 1280 | tf_op jit(solution)/shard_map/scatter | solution.py:61
  8.1 0.7 copy.33
  8.8 8.6 %all-to-all-start = ((s32[32,1,4]{2,1,0:T(1,128)}), s32[32,1,4]{2,1,0:T(1,128)S(1)}, u32[]{:S(2)}, u32[]{:S(2)}) async-start(s32[32,1,4]{2,1,0:T(1,128)} %copy.33), calls=%async_computation | async-start | bytes 32768 | tf_op jit(solution)/shard_map/all_to_all | solution.py:64
  17.4 9.1 %fusion = bf16[8,8,8,8,128]{4,3,2,1,0:T(8,128)(2,1)S(1)} fusion(bf16[8,64,1024]{2,1,0:T(8,128)(2,1)} %param.7, bf16[8,1024,1024]{2,1,0:T(8,128)(2,1)} %param.8), kind=kOutput, calls=%fused_computation.11 | convolution fusion | flops 1074266112 | bytes 18874368 | tf_op jit(solution)/shard_map/skl,slm->skm/dot_general | solution.py:10
  26.5 0.3 copy.63
  26.8 1.9 broadcast.81.clone
  28.7 8.9 %scatter_fusion.1 = bf16[32,4,64,128]{3,2,1,0:T(8,128)(2,1)} fusion(bf16[32,4,64,128]{3,2,1,0:T(8,128)(2,1)} %broadcast.81.clone, s32[64]{0:T(128)S(1)} %get-tuple-element.2, bf16[64,64,128]{2,1,0:T(8,128)(2,1)S(1)} %bitcast.87), kind=kCustom, calls=%fused_computation.3 | custom fusion | bytes 3146240 | tf_op jit(solution)/shard_map/scatter | solution.py:36
  37.5 0.0 copy-start.1
  37.5 0.0 all-to-all-done
  37.5 7.6 %all-to-all-start.1 = ((bf16[32,4,64,128]{3,2,1,0:T(8,128)(2,1)}), bf16[32,4,64,128]{3,2,1,0:T(8,128)(2,1)}, u32[]{:S(2)}, u32[]{:S(2)}) async-start(bf16[32,4,64,128]{3,2,1,0:T(8,128)(2,1)} %scatter_fusion.1), calls=%async_computation.1 | async-start | bytes 4194304 | tf_op jit(solution)/shard_map/all_to_all | solution.py:63
  45.1 0.0 copy-done.1
  45.1 0.5 broadcast.184
  45.7 0.7 reduce.3
  46.4 0.1 reshape.115
  46.5 0.1 copy.37
  46.5 0.1 copy.38
  46.6 0.1 reshape.129
  46.8 26.7 %all-to-all-done.1 = bf16[32,4,64,128]{3,2,1,0:T(8,128)(2,1)} async-done(((bf16[32,4,64,128]{3,2,1,0:T(8,128)(2,1)}), bf16[32,4,64,128]{3,2,1,0:T(8,128)(2,1)}, u32[]{:S(2)}, u32[]{:S(2)}) %all-to-all-start.1) | async-done | bytes 2097184 | tf_op jit(solution)/shard_map/all_to_all | solution.py:63
  73.5 4.0 %bitcast_convert_fusion.1 = f32[128,64,128]{2,1,0:T(8,128)} fusion(bf16[32,4,64,128]{3,2,1,0:T(8,128)(2,1)} %all-to-all-done.1), kind=kLoop, calls=%fused_computation.8 | loop fusion | flops 1048576 | bytes 6291456 | tf_op jit(solution)/shard_map/convert_element_type | solution.py:41
  77.5 13.5 %scatter_fusion.2 = f32[16,64,128]{2,1,0:T(8,128)S(1)} fusion(f32[16,64,128]{2,1,0:T(8,128)S(1)} %broadcast.74.clone, s32[128]{0:T(128)S(1)} %fusion.14, f32[128,64,128]{2,1,0:T(8,128)} %bitcast_convert_fusion.1), kind=kCustom, calls=%fused_computation.4 | custom fusion | flops 1048576 | bytes 12583424 | tf_op jit(solution)/shard_map/scatter-add | solution.py:42
  91.1 3.0 fusion.7
  94.1 121.1 %all-reduce.1 = bf16[64,1024]{1,0:T(8,128)(2,1)S(1)} all-reduce(f32[64,1024]{1,0:T(8,128)S(1)} %fusion.7), channel_id=1, replica_groups=mesh['sub'=32,'rep'=4] {'sub'}, use_global_device_ids=true, to_apply=%region_4.0 | all-reduce | flops 65536 | bytes 393216 | tf_op jit(solution)/shard_map/psum | solution.py:68
  215.3 0.0 copy-done
  215.3 4.8 %fusion.2 = f32[64,2048]{1,0:T(8,128)} fusion(bf16[2048,1024]{1,0:T(8,128)(2,1)} %param.12, bf16[1024,1024]{1,0:T(8,128)(2,1)S(1)} %copy-done, bf16[64,1024]{1,0:T(8,128)(2,1)S(1)} %all-reduce.1), kind=kOutput, calls=%fused_computation.14 | convolution fusion | flops 402718720 | bytes 6946816 | tf_op jit(solution)/shard_map/dot_general | solution.py:72
  220.0 1.1 bitcast_bitcast_fusion
  221.1 2.1 gather_fusion
  223.2 38.3 %all_to_all.27 = bf16[32,4,64,128]{3,2,1,0:T(8,128)(2,1)} all-to-all(bf16[32,4,64,128]{3,2,1,0:T(8,128)(2,1)} %bitcast.85), channel_id=1, replica_groups=mesh['sub'=32,'rep'=4] {'sub'}, dimensions={0} | all-to-all | bytes 4194304 | tf_op jit(solution)/shard_map/all_to_all | solution.py:78
  261.5 3.3 gather_fusion.1
  264.8 9.1 %fusion.1 = bf16[8,8,8,8,128]{4,3,2,1,0:T(8,128)(2,1)S(1)} fusion(bf16[8,1024,1024]{2,1,0:T(8,128)(2,1)} %param.8, bf16[8,8,8,8,128]{4,3,2,1,0:T(8,128)(2,1)} %bitcast.88), kind=kOutput, calls=%fused_computation.12 | convolution fusion | flops 1074266112 | bytes 18874368 | tf_op jit(solution)/shard_map/skl,slm->skm/dot_general | solution.py:10
  273.9 1.3 copy.62
  275.2 1.9 broadcast.81
  277.1 9.8 %scatter_fusion.3 = bf16[32,4,64,128]{3,2,1,0:T(8,128)(2,1)} fusion(bf16[32,4,64,128]{3,2,1,0:T(8,128)(2,1)} %broadcast.81, s32[64]{0:T(128)S(1)} %get-tuple-element.2, bf16[64,64,128]{2,1,0:T(8,128)(2,1)} %bitcast.86), kind=kCustom, calls=%fused_computation.5 | custom fusion | bytes 3146240 | tf_op jit(solution)/shard_map/scatter | solution.py:36
  286.9 32.1 %all_to_all.28 = bf16[32,4,64,128]{3,2,1,0:T(8,128)(2,1)S(1)} all-to-all(bf16[32,4,64,128]{3,2,1,0:T(8,128)(2,1)} %scatter_fusion.3), channel_id=1, replica_groups=mesh['sub'=32,'rep'=4] {'sub'}, dimensions={0} | all-to-all | bytes 4194304 | tf_op jit(solution)/shard_map/all_to_all | solution.py:82
  319.0 2.5 bitcast_convert_fusion
  321.6 13.5 %scatter_fusion.4 = f32[16,64,128]{2,1,0:T(8,128)S(1)} fusion(f32[16,64,128]{2,1,0:T(8,128)S(1)} %broadcast.74, s32[128]{0:T(128)S(1)} %fusion.14, f32[128,64,128]{2,1,0:T(8,128)} %bitcast_convert_fusion), kind=kCustom, calls=%fused_computation.6 | custom fusion | flops 1048576 | bytes 12583424 | tf_op jit(solution)/shard_map/scatter-add | solution.py:42
  335.1 0.9 fusion.5
  (7 shorter events, 0.1 us)
Async XLA Ops:
  0.6 214.6 %copy-start = (bf16[1024,1024]{1,0:T(8,128)(2,1)S(1)}, bf16[1024,1024]{1,0:T(8,128)(2,1)}, u32[]{:S(2)}) copy-start(bf16[1024,1024]{1,0:T(8,128)(2,1)} %param.13) | copy-start | bytes 6291460
  8.8 28.8 %all-to-all-start = ((s32[32,1,4]{2,1,0:T(1,128)}), s32[32,1,4]{2,1,0:T(1,128)S(1)}, u32[]{:S(2)}, u32[]{:S(2)}) async-start(s32[32,1,4]{2,1,0:T(1,128)} %copy.33), calls=%async_computation | async-start | bytes 32768 | tf_op jit(solution)/shard_map/all_to_all | solution.py:64
  37.5 7.6 %copy-start.1 = (s32[2048]{0:T(1024)S(1)}, s32[2048]{0:T(1024)}, u32[]{:S(2)}) copy-start(s32[2048]{0:T(1024)} %param.11) | copy-start | bytes 24580
  37.5 35.9 %all-to-all-start.1 = ((bf16[32,4,64,128]{3,2,1,0:T(8,128)(2,1)}), bf16[32,4,64,128]{3,2,1,0:T(8,128)(2,1)}, u32[]{:S(2)}, u32[]{:S(2)}) async-start(bf16[32,4,64,128]{3,2,1,0:T(8,128)(2,1)} %scatter_fusion.1), calls=%async_computation.1 | async-start | bytes 4194304 | tf_op jit(solution)/shard_map/all_to_all | solution.py:63
where the time goes:
time: 338 us; the launch traced here: 336 us
  blocking collectives  192 us (57%)
  other arithmetic  37.9 us (11%)
  local copies, waits for them, and re-layouts  36.8 us (11%)
  waiting for transfers between devices  26.7 us (8%)
  matrix products  26.1 us (8%)
  starting transfers between devices  16.2 us (5%)
    psum x1, blocking collectives, per_device(): summed = lax.psum(coeff, 'sub')  121 us
    all_to_all x1, blocking collectives, per_device(): lax.all_to_all(requested, 'sub', split_axis=0, concat_axis=0, tiled=True)  38.3 us
    all_to_all x1, blocking collectives, per_device(): lax.all_to_all(pack_slots(make_blocks(again, width), dests, ranks, peers,...  32.1 us
    scatter-add x2, other arithmetic, accumulate(): jnp.zeros((own_blocks, columns, width), jnp.float32).at[got_ids.reshape(-1)]  27.1 us
    all_to_all x1, waiting for transfers between devices, per_device(): lax.all_to_all(packed, 'sub', split_axis=0, concat_axis=0, tiled=True)  26.7 us
    scatter x2, local copies, waits for them, and re-layouts, pack_slots(): jnp.zeros((peers, slots, columns, width), jnp.bfloat16).at[dests, ranks]  18.7 us
    dot_general x2, matrix products, apply_local(): jnp.einsum('skl,slm->skm', inputs, operators, preferred_element_type=jnp....  18.3 us
    all_to_all x1, starting transfers between devices, per_device(): lax.all_to_all(id_slots, 'sub', split_axis=0, concat_axis=0, tiled=True)  8.59 us
  transfers between devices with their start and end apart: 2, of which 1 were waited for; matrix products, arithmetic and copies ran while one was open for 6% of the time, Pallas kernels for 0%

commit v1 on v0

--- a/solution.py
+++ b/solution.py
@@ -65,7 +65,9 @@
     )
     dual = accumulate(received, got_ids, own_blocks, weight)
     coeff = jnp.dot(dual.astype(jnp.bfloat16), basis, preferred_element_type=jnp.float32)
-    summed = lax.psum(coeff, "sub")
+    summed = coeff
+    for hop in (1, 2, 4, 8, 16):
+        summed = summed + lax.ppermute(summed, "sub", [(dev, dev ^ hop) for dev in range(32)])
     solved = jnp.dot(
         summed.astype(jnp.bfloat16), coarse, preferred_element_type=jnp.float32
     ).astype(jnp.bfloat16)

time: 338 us -> 246 us (0.73)
  blocking collectives: 192 us -> 69.4 us
  waiting for transfers between devices: 26.7 us -> 54.2 us
    psum x1 -> x0, blocking collectives: 121 us -> none  [per_device(): summed = lax.psum(coeff, 'sub')]
    ppermute x0 -> x5, waiting for transfers between devices: none -> 27.2 us  [per_device(): lax.ppermute(summed, 'sub', [(dev, dev ^ hop) for dev in range(32)])]
  transfers between devices with their start and end apart: 2 -> 7, of which waited for: 1 -> 6; matrix products, arithmetic and copies ran while one was open for 6% -> 10% of each run, Pallas kernels for 0% -> 0%
where the time goes in v1:
time: 246 us; the launch traced here: 245 us
  blocking collectives  69.4 us (28%)
  waiting for transfers between devices  54.2 us (22%)
  local copies, waits for them, and re-layouts  38.8 us (16%)
  other arithmetic  37 us (15%)
  matrix products  25.3 us (10%)
  starting transfers between devices  19.2 us (8%)
    all_to_all x1, blocking collectives, per_device(): lax.all_to_all(requested, 'sub', split_axis=0, concat_axis=0, tiled=True)  37.3 us
    all_to_all x1, blocking collectives, per_device(): lax.all_to_all(pack_slots(make_blocks(again, width), dests, ranks, peers,...  32.1 us
    ppermute x5, waiting for transfers between devices, per_device(): lax.ppermute(summed, 'sub', [(dev, dev ^ hop) for dev in range(32)])  27.2 us
    scatter-add x2, other arithmetic, accumulate(): jnp.zeros((own_blocks, columns, width), jnp.float32).at[got_ids.reshape(-1)]  27.1 us
    all_to_all x1, waiting for transfers between devices, per_device(): lax.all_to_all(packed, 'sub', split_axis=0, concat_axis=0, tiled=True)  27 us
    scatter x2, local copies, waits for them, and re-layouts, pack_slots(): jnp.zeros((peers, slots, columns, width), jnp.bfloat16).at[dests, ranks]  19.6 us
    dot_general x2, matrix products, apply_local(): jnp.einsum('skl,slm->skm', inputs, operators, preferred_element_type=jnp....  18.3 us
    all_to_all x1, starting transfers between devices, per_device(): lax.all_to_all(id_slots, 'sub', split_axis=0, concat_axis=0, tiled=True)  8.59 us
  transfers between devices with their start and end apart: 7, of which 6 were waited for; matrix products, arithmetic and copies ran while one was open for 10% of the time, Pallas kernels for 0%

profile of v1, /device:TPU:1, one launch (start us, length us, event | category | flops | bytes accessed | tf_op | source)
XLA Modules:
  0.0 244.7 jit_solution(18135359633866559109)
XLA Ops:
  0.6 0.0 copy-start
  0.6 1.0 convert_reduce_fusion
  1.6 0.7 fusion.13
  2.3 5.7 %scatter_fusion = s32[32,4]{0,1:T(4,128)S(1)} fusion(s32[32,4]{0,1:T(4,128)S(1)} %broadcast.75, s32[64]{0:T(128)S(1)} %get-tuple-element.2, s32[64]{0:T(128)} %param.10), kind=kCustom, calls=%fused_computation.2 | custom fusion | bytes 1280 | tf_op jit(solution)/shard_map/scatter | solution.py:61
  8.1 0.7 copy.33
  8.8 8.6 %all-to-all-start = ((s32[32,1,4]{2,1,0:T(1,128)}), s32[32,1,4]{2,1,0:T(1,128)S(1)}, u32[]{:S(2)}, u32[]{:S(2)}) async-start(s32[32,1,4]{2,1,0:T(1,128)} %copy.33), calls=%async_computation | async-start | bytes 32768 | tf_op jit(solution)/shard_map/all_to_all | solution.py:64
  17.4 9.1 %fusion = bf16[8,8,8,8,128]{4,3,2,1,0:T(8,128)(2,1)S(1)} fusion(bf16[8,64,1024]{2,1,0:T(8,128)(2,1)} %param.7, bf16[8,1024,1024]{2,1,0:T(8,128)(2,1)} %param.8), kind=kOutput, calls=%fused_computation.11 | convolution fusion | flops 1074266112 | bytes 18874368 | tf_op jit(solution)/shard_map/skl,slm->skm/dot_general | solution.py:10
  26.5 1.3 copy.63
  27.8 1.9 broadcast.81.clone
  29.6 9.8 %scatter_fusion.1 = bf16[32,4,64,128]{3,2,1,0:T(8,128)(2,1)} fusion(bf16[32,4,64,128]{3,2,1,0:T(8,128)(2,1)} %broadcast.81.clone, s32[64]{0:T(128)S(1)} %get-tuple-element.2, bf16[64,64,128]{2,1,0:T(8,128)(2,1)} %bitcast.86), kind=kCustom, calls=%fused_computation.3 | custom fusion | bytes 3146240 | tf_op jit(solution)/shard_map/scatter | solution.py:36
  39.5 0.0 all-to-all-done
  39.5 7.6 %all-to-all-start.1 = ((bf16[32,4,64,128]{3,2,1,0:T(8,128)(2,1)}), bf16[32,4,64,128]{3,2,1,0:T(8,128)(2,1)}, u32[]{:S(2)}, u32[]{:S(2)}) async-start(bf16[32,4,64,128]{3,2,1,0:T(8,128)(2,1)} %scatter_fusion.1), calls=%async_computation.1 | async-start | bytes 4194304 | tf_op jit(solution)/shard_map/all_to_all | solution.py:63
  47.1 0.0 copy-done.2
  47.1 0.5 broadcast.184
  47.6 0.7 reduce.3
  48.3 0.1 reshape.115
  48.4 27.0 %all-to-all-done.1 = bf16[32,4,64,128]{3,2,1,0:T(8,128)(2,1)} async-done(((bf16[32,4,64,128]{3,2,1,0:T(8,128)(2,1)}), bf16[32,4,64,128]{3,2,1,0:T(8,128)(2,1)}, u32[]{:S(2)}, u32[]{:S(2)}) %all-to-all-start.1) | async-done | bytes 2097184 | tf_op jit(solution)/shard_map/all_to_all | solution.py:63
  75.4 4.0 %bitcast_convert_fusion.1 = f32[128,64,128]{2,1,0:T(8,128)} fusion(bf16[32,4,64,128]{3,2,1,0:T(8,128)(2,1)} %all-to-all-done.1), kind=kLoop, calls=%fused_computation.8 | loop fusion | flops 1048576 | bytes 6291456 | tf_op jit(solution)/shard_map/convert_element_type | solution.py:41
  79.4 13.5 %scatter_fusion.2 = f32[16,64,128]{2,1,0:T(8,128)S(1)} fusion(f32[16,64,128]{2,1,0:T(8,128)S(1)} %broadcast.74.clone, s32[128]{0:T(128)S(1)} %fusion.12, f32[128,64,128]{2,1,0:T(8,128)} %bitcast_convert_fusion.1), kind=kCustom, calls=%fused_computation.4 | custom fusion | flops 1048576 | bytes 12583424 | tf_op jit(solution)/shard_map/scatter-add | solution.py:42
  93.0 3.0 %fusion.7 = f32[64,1024]{1,0:T(8,128)S(1)} fusion(bf16[2048,1024]{1,0:T(8,128)(2,1)} %param.12, f32[2048]{0:T(1024)S(1)} %add_divide_fusion, f32[16,64,128]{2,1,0:T(8,128)S(1)} %scatter_fusion.2), kind=kOutput, calls=%fused_computation.23 | convolution fusion | flops 268697600 | bytes 4988928 | tf_op jit(solution)/shard_map/dot_general | solution.py:67
  96.0 0.9 collective-permute-start
  97.0 1.2 collective-permute-done
  98.2 0.1 collective-permute-start.1
  98.3 7.5 %collective-permute-done.1 = f32[64,1024]{1,0:T(8,128)S(1)} collective-permute-done((f32[64,1024]{1,0:T(8,128)S(1)}, f32[64,1024]{1,0:T(8,128)S(1)}, u32[]{:S(2)}, u32[]{:S(2)}) %collective-permute-start.1) | collective-permute-done | bytes 262176 | tf_op jit(solution)/shard_map/ppermute | solution.py:70
  105.8 0.7 collective-permute-start.2
  106.5 7.5 %collective-permute-done.2 = f32[64,1024]{1,0:T(8,128)S(1)} collective-permute-done((f32[64,1024]{1,0:T(8,128)S(1)}, f32[64,1024]{1,0:T(8,128)S(1)}, u32[]{:S(2)}, u32[]{:S(2)}) %collective-permute-start.2) | collective-permute-done | bytes 262176 | tf_op jit(solution)/shard_map/ppermute | solution.py:70
  114.0 0.1 collective-permute-start.3
  114.1 0.1 copy.37
  114.2 5.6 %collective-permute-done.3 = f32[64,1024]{1,0:T(8,128)S(1)} collective-permute-done((f32[64,1024]{1,0:T(8,128)S(1)}, f32[64,1024]{1,0:T(8,128)S(1)}, u32[]{:S(2)}, u32[]{:S(2)}) %collective-permute-start.3) | collective-permute-done | bytes 262176 | tf_op jit(solution)/shard_map/ppermute | solution.py:70
  119.8 1.2 collective-permute-start.4
  121.0 0.1 copy.38
  121.1 0.1 reshape.129
  121.2 5.5 %collective-permute-done.4 = f32[64,1024]{1,0:T(8,128)} collective-permute-done((f32[64,1024]{1,0:T(8,128)S(1)}, f32[64,1024]{1,0:T(8,128)}, u32[]{:S(2)}, u32[]{:S(2)}) %collective-permute-start.4) | collective-permute-done | bytes 262176 | tf_op jit(solution)/shard_map/ppermute | solution.py:70
  126.7 0.0 copy-done
  126.7 4.1 %fusion.2 = f32[64,2048]{1,0:T(8,128)S(1)} fusion(bf16[2048,1024]{1,0:T(8,128)(2,1)} %param.12, bf16[1024,1024]{1,0:T(8,128)(2,1)S(1)} %copy-done, f32[64,1024]{1,0:T(8,128)S(1)} %add.73, f32[64,1024]{1,0:T(8,128)} %collective-permute-done.4), kind=kOutput, calls=%fused_computation.14 | convolution fusion | flops 402849792 | bytes 7340032 | tf_op jit(solution)/shard_map/dot_general | solution.py:74
  130.8 0.0 copy-start.1
  130.9 2.1 gather_fusion
  133.0 0.0 copy-done.1
  133.0 37.3 %all_to_all.27 = bf16[32,4,64,128]{3,2,1,0:T(8,128)(2,1)} all-to-all(bf16[32,4,64,128]{3,2,1,0:T(8,128)(2,1)} %bitcast.84), channel_id=1, replica_groups=mesh['sub'=32,'rep'=4] {'sub'}, dimensions={0} | all-to-all | bytes 4194304 | tf_op jit(solution)/shard_map/all_to_all | solution.py:80
  170.3 3.3 %gather_fusion.1 = bf16[64,64,128]{2,1,0:T(8,128)(2,1)} fusion(bf16[32,4,64,128]{3,2,1,0:T(8,128)(2,1)} %all_to_all.27, s32[64]{0:T(128)S(1)} %bitcast.88), kind=kCustom, calls=%fused_computation.1 | custom fusion | bytes 2097664 | tf_op jit(solution)/shard_map/gather | solution.py:81
  173.6 9.1 %fusion.1 = bf16[8,8,8,8,128]{4,3,2,1,0:T(8,128)(2,1)S(1)} fusion(bf16[8,1024,1024]{2,1,0:T(8,128)(2,1)} %param.8, bf16[8,8,8,8,128]{4,3,2,1,0:T(8,128)(2,1)} %bitcast.87), kind=kOutput, calls=%fused_computation.12 | convolution fusion | flops 1074266112 | bytes 18874368 | tf_op jit(solution)/shard_map/skl,slm->skm/dot_general | solution.py:10
  182.7 1.3 copy.62
  184.0 1.9 broadcast.81
  185.8 9.8 %scatter_fusion.3 = bf16[32,4,64,128]{3,2,1,0:T(8,128)(2,1)} fusion(bf16[32,4,64,128]{3,2,1,0:T(8,128)(2,1)} %broadcast.81, s32[64]{0:T(128)S(1)} %get-tuple-element.2, bf16[64,64,128]{2,1,0:T(8,128)(2,1)} %bitcast.85), kind=kCustom, calls=%fused_computation.5 | custom fusion | bytes 3146240 | tf_op jit(solution)/shard_map/scatter | solution.py:36
  195.7 32.1 %all_to_all.28 = bf16[32,4,64,128]{3,2,1,0:T(8,128)(2,1)S(1)} all-to-all(bf16[32,4,64,128]{3,2,1,0:T(8,128)(2,1)} %scatter_fusion.3), channel_id=1, replica_groups=mesh['sub'=32,'rep'=4] {'sub'}, dimensions={0} | all-to-all | bytes 4194304 | tf_op jit(solution)/shard_map/all_to_all | solution.py:84
  227.7 2.5 %bitcast_convert_fusion = f32[128,64,128]{2,1,0:T(8,128)} fusion(bf16[32,4,64,128]{3,2,1,0:T(8,128)(2,1)S(1)} %all_to_all.28), kind=kLoop, calls=%fused_computation.7 | loop fusion | flops 1048576 | bytes 6291456 | tf_op jit(solution)/shard_map/convert_element_type | solution.py:41
  230.3 13.5 %scatter_fusion.4 = f32[16,64,128]{2,1,0:T(8,128)S(1)} fusion(f32[16,64,128]{2,1,0:T(8,128)S(1)} %broadcast.74, s32[128]{0:T(128)S(1)} %fusion.12, f32[128,64,128]{2,1,0:T(8,128)} %bitcast_convert_fusion), kind=kCustom, calls=%fused_computation.6 | custom fusion | flops 1048576 | bytes 12583424 | tf_op jit(solution)/shard_map/scatter-add | solution.py:42
  243.9 0.9 fusion.5
  (13 shorter events, 0.3 us)
Async XLA Ops:
  0.6 126.1 %copy-start = (bf16[1024,1024]{1,0:T(8,128)(2,1)S(1)}, bf16[1024,1024]{1,0:T(8,128)(2,1)}, u32[]{:S(2)}) copy-start(bf16[1024,1024]{1,0:T(8,128)(2,1)} %param.13) | copy-start | bytes 6291460
  8.8 30.7 %all-to-all-start = ((s32[32,1,4]{2,1,0:T(1,128)}), s32[32,1,4]{2,1,0:T(1,128)S(1)}, u32[]{:S(2)}, u32[]{:S(2)}) async-start(s32[32,1,4]{2,1,0:T(1,128)} %copy.33), calls=%async_computation | async-start | bytes 32768 | tf_op jit(solution)/shard_map/all_to_all | solution.py:64
  39.5 7.6 %copy-start.2 = (s32[2048]{0:T(1024)S(1)}, s32[2048]{0:T(1024)}, u32[]{:S(2)}) copy-start(s32[2048]{0:T(1024)} %param.11) | copy-start | bytes 24580
  39.5 35.9 %all-to-all-start.1 = ((bf16[32,4,64,128]{3,2,1,0:T(8,128)(2,1)}), bf16[32,4,64,128]{3,2,1,0:T(8,128)(2,1)}, u32[]{:S(2)}, u32[]{:S(2)}) async-start(bf16[32,4,64,128]{3,2,1,0:T(8,128)(2,1)} %scatter_fusion.1), calls=%async_computation.1 | async-start | bytes 4194304 | tf_op jit(solution)/shard_map/all_to_all | solution.py:63
  96.0 2.1 collective-permute-start
  98.2 7.6 %collective-permute-start.1 = (f32[64,1024]{1,0:T(8,128)S(1)}, f32[64,1024]{1,0:T(8,128)S(1)}, u32[]{:S(2)}, u32[]{:S(2)}) collective-permute-start(f32[64,1024]{1,0:T(8,128)S(1)} %add.70), channel_id=1, source_target_pairs={{0,8},{4,12},{8,0},{12,4},{16,24},{20,28},{24,16},{28,20},{32,40},... | collective-permute-start | bytes 786440 | tf_op jit(solution)/shard_map/ppermute | solution.py:70
  105.8 8.2 %collective-permute-start.2 = (f32[64,1024]{1,0:T(8,128)S(1)}, f32[64,1024]{1,0:T(8,128)S(1)}, u32[]{:S(2)}, u32[]{:S(2)}) collective-permute-start(f32[64,1024]{1,0:T(8,128)S(1)} %add.71), channel_id=1, source_target_pairs={{0,16},{4,20},{8,24},{12,28},{16,0},{20,4},{24,8},{28,12},{32,48},... | collective-permute-start | bytes 786440 | tf_op jit(solution)/shard_map/ppermute | solution.py:70
  114.0 5.8 %collective-permute-start.3 = (f32[64,1024]{1,0:T(8,128)S(1)}, f32[64,1024]{1,0:T(8,128)S(1)}, u32[]{:S(2)}, u32[]{:S(2)}) collective-permute-start(f32[64,1024]{1,0:T(8,128)S(1)} %add.72), channel_id=1, source_target_pairs={{0,32},{4,36},{8,40},{12,44},{16,48},{20,52},{24,56},{28,60},{32,0... | collective-permute-start | bytes 786440 | tf_op jit(solution)/shard_map/ppermute | solution.py:70
  119.8 6.9 %collective-permute-start.4 = (f32[64,1024]{1,0:T(8,128)S(1)}, f32[64,1024]{1,0:T(8,128)}, u32[]{:S(2)}, u32[]{:S(2)}) collective-permute-start(f32[64,1024]{1,0:T(8,128)S(1)} %add.73), channel_id=1, source_target_pairs={{0,64},{4,68},{8,72},{12,76},{16,80},{20,84},{24,88},{28,92},{32,9... | collective-permute-start | bytes 786440 | tf_op jit(solution)/shard_map/ppermute | solution.py:70
  130.8 2.2 copy-start.1
